TPU v7x, 32 devices: a whole 2x2x4 slice. The times are simulated.
32 devices in a mesh: row: 8 (over z, y), col: 4 (over x, core).
Axes of the slice: x: 2, y: 2, z: 4, core: 2. Of those that a mesh axis runs over, the one named last changes fastest.
Arguments:
- examples: bfloat16 [8192, 1024], P('row'), may hold values from -40 to 40
- targets: float32 [8192, 64], P('row'), may hold values from -6 to 6
- landmark_rows: int32 [8192], P('col'), may hold values from 0 to 1023
- ainv: float32 [4, 8, 256, 8192], P(None, 'row', None, 'col'), as said below
- tinv_t: float32 [4, 8, 256, 8192], P(None, 'row', None, 'col'), as said below
Outputs:
- solution: float32 [8192, 64], P('col')
- weights: float32 [8192, 64], P('col')
Inputs may be any that keep to these rules, and one draw needn't show every extreme that they name: `landmark_rows`: landmark m is a row of example block ((m mod 2048) // 256); the value is its place within that block. `ainv`: the preconditioner's factor A inverse, in landmark order. `tinv_t`: the preconditioner's factor T inverse, transposed, in landmark order.
All inputs are finite; a program needn't handle non-finite values.
Results may differ from a plain program's by a relative error of at most 0.0003.
Values may be sent and summed in bfloat16 or wider, within the bound.
A program may use at most 128 MiB of HBM per device.

v0:
```python
import math
import jax
import jax.numpy as jnp
from jax import lax
from jax.sharding import PartitionSpec as P

D = 1024
ITERS = 2
LAMBDA = 0.001
EPSILON = 1e-06
HIGHEST = lax.Precision.HIGHEST


def kernel_tile(rows_data, landmarks, sq_lands):
    sq_rows = jnp.sum(jnp.square(rows_data.astype(jnp.float32)), axis=1)
    products = lax.dot_general(
        rows_data, landmarks, (((1,), (1,)), ((), ())), preferred_element_type=jnp.float32
    )
    return jnp.exp(-(sq_rows[:, None] + sq_lands[None, :] - 2.0 * products) / D)


def contract_rows(matrix, vectors):
    return lax.dot_general(
        matrix,
        vectors,
        (((0,), (0,)), ((), ())),
        precision=HIGHEST,
        preferred_element_type=jnp.float32,
    )


def times_matrix(matrix, vectors):
    return jnp.dot(matrix, vectors, precision=HIGHEST, preferred_element_type=jnp.float32)


def col_total(values):
    return lax.psum(values, "col")


def row_total(values):
    return lax.psum(values, "row")


def dot_total(values):
    return lax.psum(values, "col")


def column_sums(first, second):
    return jnp.sum(first * second, axis=0)


def shards(examples, targets, landmark_rows, ainv, tinv_t):
    row_count = lax.axis_size("row")
    total_rows = examples.shape[0] * row_count
    tile_width = landmark_rows.shape[0]
    owned_count = tile_width // row_count
    first_owned = lax.axis_index("row") * owned_count
    owned_ids = lax.dynamic_slice_in_dim(landmark_rows, first_owned, owned_count, 0)
    owned = jnp.take(examples, owned_ids, axis=0)
    landmarks = lax.all_gather(owned, "row", axis=0, tiled=True)
    sq_lands = jnp.sum(jnp.square(landmarks.astype(jnp.float32)), axis=1)
    kernel = kernel_tile(examples, landmarks, sq_lands)
    factor_a = ainv.reshape(-1, tile_width)
    factor_t = tinv_t.reshape(-1, tile_width)
    kernel_targets = row_total(contract_rows(kernel, targets))
    mixed = col_total(times_matrix(factor_t, kernel_targets))
    right_side = row_total(contract_rows(factor_a, mixed)) / math.sqrt(total_rows)
    solution = jnp.zeros(right_side.shape, jnp.float32)
    residual = right_side
    direction = right_side
    norm_now = dot_total(column_sums(residual, residual))
    for iteration in range(ITERS):
        mixed_in = col_total(times_matrix(factor_a, direction))
        lifted = row_total(contract_rows(factor_t, mixed_in))
        example_vals = lax.psum(times_matrix(kernel, lifted).astype(jnp.bfloat16), "col").astype(
            jnp.float32
        )
        local_back = contract_rows(kernel, example_vals)
        back = row_total(local_back)
        curvature = None
        lowered = col_total(times_matrix(factor_t, back))
        applied = row_total(contract_rows(factor_a, lowered / total_rows + LAMBDA * mixed_in))
        applied, curvature = (applied, curvature)
        step_size = norm_now / dot_total(column_sums(direction, applied))
        solution = solution + step_size * direction
        residual = residual - step_size * applied
        norm_next = dot_total(column_sums(residual, residual))
        direction = residual + norm_next / (norm_now + EPSILON) * direction
        norm_now = norm_next
    weights = row_total(contract_rows(factor_t, col_total(times_matrix(factor_a, solution))))
    return (solution, weights)


def solution(mesh):
    return jax.shard_map(
        shards,
        mesh=mesh,
        in_specs=(
            P("row", None),
            P("row", None),
            P("col"),
            P(None, "row", None, "col"),
            P(None, "row", None, "col"),
        ),
        out_specs=(P("col", None), P("col", None)),
        check_vma=False,
    )
```

profile of v0, /device:TPU:0, one launch (start us, length us, event | category | flops | bytes accessed | tf_op | source)
XLA Modules:
  0.0 1241.8 jit_solution(5362592691679920946)
XLA Ops:
  7.2 0.9 compare_and_fusion
  8.2 3.4 gather_fusion
  12.6 2.1 multiply_reduce_fusion.1
  14.7 74.1 %all-gather.2.cloned.1.call-done = bf16[2048,1024]{1,0:T(8,128)(2,1)} async-done(((bf16[256,1024]{1,0:T(8,128)(2,1)}), bf16[2048,1024]{1,0:T(8,128)(2,1)}) %all-gather.2.cloned.1.call-update) | async-done | bytes 4194320 | tf_op jit(solution)/shard_map/all_gather | solution.py:60
  88.8 3.1 multiply_reduce_fusion
  91.9 6.9 fusion.2
  98.8 3.2 copy-done.1
  102.0 7.7 fusion.21
  110.0 76.3 %all-reduce.19.cloned.1.call-done = f32[2048,64]{1,0:T(8,128)} async-done(((f32[2048,64]{1,0:T(8,128)}), f32[2048,64]{1,0:T(8,128)}) %all-reduce.19.cloned.1.call-update) | async-done | bytes 524304 | tf_op jit(solution)/shard_map/psum | solution.py:41
  186.3 12.7 %convolution_bitcast_fusion.11 = f32[1024,64]{0,1:T(8,128)} fusion(f32[2048,64]{1,0:T(8,128)} %all-reduce.19.cloned.1.call-done, f32[1024,2048]{1,0:T(8,128)} %bitcast.72), kind=kOutput, calls=%fused_computation.20 | convolution fusion | flops 1610612736 | bytes 9175040 | tf_op jit(solution)/shard_map/dot_general | solution.py:33
  199.1 31.7 %all-reduce.21.cloned.1.call-done = f32[1024,64]{0,1:T(8,128)} async-done(((f32[1024,64]{0,1:T(8,128)}), f32[1024,64]{0,1:T(8,128)}) %all-reduce.21.cloned.1.call-update) | async-done | bytes 262160 | tf_op jit(solution)/shard_map/psum | solution.py:37
  230.7 9.4 convolution_bitcast_fusion.5
  240.6 72.1 %all-reduce.23.cloned.1.call-done = f32[2048,64]{0,1:T(8,128)} async-done(((f32[2048,64]{0,1:T(8,128)}), f32[2048,64]{0,1:T(8,128)}) %all-reduce.23.cloned.1.call-update) | async-done | bytes 524304 | tf_op jit(solution)/shard_map/psum | solution.py:41
  312.7 12.3 convolution_bitcast_fusion.8
  325.1 31.3 %all-reduce.25.cloned.1.call-done = f32[1024,64]{0,1:T(8,128)} async-done(((f32[1024,64]{0,1:T(8,128)}), f32[1024,64]{0,1:T(8,128)}) %all-reduce.25.cloned.1.call-update) | async-done | bytes 262160 | tf_op jit(solution)/shard_map/psum | solution.py:37
  356.4 9.4 convolution_bitcast_fusion.4
  366.1 72.3 %all-reduce.27.cloned.1.call-done = f32[2048,64]{0,1:T(8,128)} async-done(((f32[2048,64]{0,1:T(8,128)}), f32[2048,64]{0,1:T(8,128)}) %all-reduce.27.cloned.1.call-update) | async-done | bytes 524304 | tf_op jit(solution)/shard_map/psum | solution.py:41
  438.4 16.3 %convolution_convert_fusion.1 = bf16[1024,64]{1,0:T(8,128)(2,1)} fusion(f32[1024,2048]{0,1:T(8,128)} %copy-done.1, f32[2048,64]{0,1:T(8,128)} %all-reduce.27.cloned.1.call-done), kind=kOutput, calls=%fused_computation.14 | convolution fusion | flops 1610678272 | bytes 9043968 | tf_op jit(solution)/shard_map/dot_general | solution.py:33
  454.8 31.4 %all-reduce.29.cloned.1.call-done = bf16[1024,64]{1,0:T(8,128)(2,1)} async-done(((bf16[1024,64]{1,0:T(8,128)(2,1)}), bf16[1024,64]{1,0:T(8,128)(2,1)}) %all-reduce.29.cloned.1.call-update) | async-done | bytes 131088 | tf_op jit(solution)/shard_map/psum | solution.py:75
  486.1 8.2 fusion.22
  494.7 78.0 %all-reduce.31.cloned.1.call-done = f32[2048,64]{1,0:T(8,128)} async-done(((f32[2048,64]{1,0:T(8,128)}), f32[2048,64]{1,0:T(8,128)}) %all-reduce.31.cloned.1.call-update) | async-done | bytes 524304 | tf_op jit(solution)/shard_map/psum | solution.py:41
  572.7 12.7 %convolution_bitcast_fusion.10 = f32[1024,64]{0,1:T(8,128)} fusion(f32[2048,64]{1,0:T(8,128)} %all-reduce.31.cloned.1.call-done, f32[1024,2048]{1,0:T(8,128)} %bitcast.74), kind=kOutput, calls=%fused_computation.19 | convolution fusion | flops 1610612736 | bytes 9175040 | tf_op jit(solution)/shard_map/dot_general | solution.py:33
  585.5 31.6 %all-reduce.33.cloned.1.call-done = f32[1024,64]{0,1:T(8,128)} async-done(((f32[1024,64]{0,1:T(8,128)}), f32[1024,64]{0,1:T(8,128)}) %all-reduce.33.cloned.1.call-update) | async-done | bytes 262160 | tf_op jit(solution)/shard_map/psum | solution.py:37
  617.2 9.4 convolution_bitcast_fusion.3
  626.6 72.5 %all-reduce.35.cloned.1.call-done = f32[2048,64]{0,1:T(8,128)} async-done(((f32[2048,64]{0,1:T(8,128)}), f32[2048,64]{0,1:T(8,128)}) %all-reduce.35.cloned.1.call-update) | async-done | bytes 524304 | tf_op jit(solution)/shard_map/psum | solution.py:41
  699.1 1.2 multiply_reduce_fusion.4
  700.3 5.7 all-reduce
  706.0 1.3 multiply_reduce_fusion.3
  707.3 7.0 psum.158
  714.3 12.4 convolution_bitcast_fusion.7
  726.8 30.8 %all-reduce.37.cloned.1.call-done = f32[1024,64]{0,1:T(8,128)} async-done(((f32[1024,64]{0,1:T(8,128)}), f32[1024,64]{0,1:T(8,128)}) %all-reduce.37.cloned.1.call-update) | async-done | bytes 262160 | tf_op jit(solution)/shard_map/psum | solution.py:37
  757.6 9.4 convolution_bitcast_fusion.2
  767.2 72.2 %all-reduce.39.cloned.1.call-done = f32[2048,64]{0,1:T(8,128)} async-done(((f32[2048,64]{0,1:T(8,128)}), f32[2048,64]{0,1:T(8,128)}) %all-reduce.39.cloned.1.call-update) | async-done | bytes 524304 | tf_op jit(solution)/shard_map/psum | solution.py:41
  839.5 16.3 %convolution_convert_fusion = bf16[1024,64]{1,0:T(8,128)(2,1)} fusion(f32[1024,2048]{0,1:T(8,128)} %copy-done.1, f32[2048,64]{0,1:T(8,128)} %all-reduce.39.cloned.1.call-done), kind=kOutput, calls=%fused_computation.13 | convolution fusion | flops 1610678272 | bytes 9043968 | tf_op jit(solution)/shard_map/dot_general | solution.py:33
  855.9 31.4 %all-reduce.41.cloned.1.call-done = bf16[1024,64]{1,0:T(8,128)(2,1)} async-done(((bf16[1024,64]{1,0:T(8,128)(2,1)}), bf16[1024,64]{1,0:T(8,128)(2,1)}) %all-reduce.41.cloned.1.call-update) | async-done | bytes 131088 | tf_op jit(solution)/shard_map/psum | solution.py:75
  887.2 8.2 fusion.23
  895.8 78.0 %all-reduce.43.cloned.1.call-done = f32[2048,64]{1,0:T(8,128)} async-done(((f32[2048,64]{1,0:T(8,128)}), f32[2048,64]{1,0:T(8,128)}) %all-reduce.43.cloned.1.call-update) | async-done | bytes 524304 | tf_op jit(solution)/shard_map/psum | solution.py:41
  973.8 12.7 %convolution_bitcast_fusion.9 = f32[1024,64]{0,1:T(8,128)} fusion(f32[2048,64]{1,0:T(8,128)} %all-reduce.43.cloned.1.call-done, f32[1024,2048]{1,0:T(8,128)} %bitcast.76), kind=kOutput, calls=%fused_computation.18 | convolution fusion | flops 1610612736 | bytes 9175040 | tf_op jit(solution)/shard_map/dot_general | solution.py:33
  986.6 31.7 %all-reduce.45.cloned.1.call-done = f32[1024,64]{0,1:T(8,128)} async-done(((f32[1024,64]{0,1:T(8,128)}), f32[1024,64]{0,1:T(8,128)}) %all-reduce.45.cloned.1.call-update) | async-done | bytes 262160 | tf_op jit(solution)/shard_map/psum | solution.py:37
  1018.2 9.4 convolution_bitcast_fusion.1
  1027.7 72.5 %all-reduce.47.cloned.1.call-done = f32[2048,64]{0,1:T(8,128)} async-done(((f32[2048,64]{0,1:T(8,128)}), f32[2048,64]{0,1:T(8,128)}) %all-reduce.47.cloned.1.call-update) | async-done | bytes 524304 | tf_op jit(solution)/shard_map/psum | solution.py:41
  1100.2 1.3 multiply_reduce_fusion.2
  1101.6 5.9 psum.165
  1107.8 11.3 convolution_bitcast_fusion.6
  1119.1 31.5 %all-reduce.49.cloned.1.call-done = f32[1024,64]{0,1:T(8,128)} async-done(((f32[1024,64]{0,1:T(8,128)}), f32[1024,64]{0,1:T(8,128)}) %all-reduce.49.cloned.1.call-update) | async-done | bytes 262160 | tf_op jit(solution)/shard_map/psum | solution.py:37
  1150.7 9.4 convolution_bitcast_fusion
  1160.1 72.6 %all-reduce.51.cloned.1.call-done = f32[2048,64]{0,1:T(8,128)} async-done(((f32[2048,64]{0,1:T(8,128)}), f32[2048,64]{0,1:T(8,128)}) %all-reduce.51.cloned.1.call-update) | async-done | bytes 524304 | tf_op jit(solution)/shard_map/psum | solution.py:41
  1232.7 1.9 copy.24
  (57 shorter events, 3.7 us)
Async XLA Ops:
  7.2 94.8 %copy-start = (f32[1024,64]{0,1:T(8,128)S(1)}, f32[1024,64]{0,1:T(8,128)}, u32[]{:S(2)}) copy-start(f32[1024,64]{0,1:T(8,128)} %param.6) | copy-start | bytes 786436
  7.2 84.7 %copy-start.3 = (bf16[1024,1024]{1,0:T(8,128)(2,1)S(1)}, bf16[1024,1024]{1,0:T(8,128)(2,1)}, u32[]{:S(2)}) copy-start(bf16[1024,1024]{1,0:T(8,128)(2,1)} %param.5) | copy-start | bytes 6291460
  7.2 81.6 %all-gather.2.cloned.1.call-start = ((), (), s32[]{:S(2)}) async-start(), calls=%async_computation | async-start | bytes 4718592 | tf_op jit(solution)/shard_map/all_gather | solution.py:60
  12.5 173.8 %all-reduce.19.cloned.1.call-start = ((), (), s32[]{:S(2)}) async-start(), calls=%async_computation.1 | async-start | bytes 2097152 | tf_op jit(solution)/shard_map/psum | solution.py:41
  98.7 3.2 copy-start.1
  109.7 121.0 %all-reduce.21.cloned.1.call-start = ((), (), s32[]{:S(2)}) async-start(), calls=%async_computation.2 | async-start | bytes 524288 | tf_op jit(solution)/shard_map/psum | solution.py:37
  199.0 113.7 %all-reduce.23.cloned.1.call-start = ((), (), s32[]{:S(2)}) async-start(), calls=%async_computation.3 | async-start | bytes 1048576 | tf_op jit(solution)/shard_map/psum | solution.py:41
  240.2 116.2 %all-reduce.25.cloned.1.call-start = ((), (), s32[]{:S(2)}) async-start(), calls=%async_computation.4 | async-start | bytes 524288 | tf_op jit(solution)/shard_map/psum | solution.py:37
  325.0 113.4 %all-reduce.27.cloned.1.call-start = ((), (), s32[]{:S(2)}) async-start(), calls=%async_computation.5 | async-start | bytes 1048576 | tf_op jit(solution)/shard_map/psum | solution.py:41
  365.8 120.3 %all-reduce.29.cloned.1.call-start = ((), (), s32[]{:S(2)}) async-start(), calls=%async_computation.6 | async-start | bytes 524288 | tf_op jit(solution)/shard_map/psum | solution.py:75
  454.7 162.4 %copy-start.7 = (f32[1024,64]{0,1:T(8,128)S(1)}, f32[1024,64]{0,1:T(8,128)}, u32[]{:S(2)}) copy-start(f32[1024,64]{0,1:T(8,128)} %all-reduce.25.cloned.1.call-done) | copy-start | bytes 786436
  454.7 118.0 %all-reduce.31.cloned.1.call-start = ((), (), s32[]{:S(2)}) async-start(), calls=%async_computation.7 | async-start | bytes 2097152 | tf_op jit(solution)/shard_map/psum | solution.py:41
  494.4 204.7 %copy-start.2 = (f32[2048,64]{0,1:T(8,128)S(1)}, f32[2048,64]{0,1:T(8,128)}, u32[]{:S(2)}) copy-start(f32[2048,64]{0,1:T(8,128)} %all-reduce.23.cloned.1.call-done) | copy-start | bytes 1572868
  494.4 122.8 %all-reduce.33.cloned.1.call-start = ((), (), s32[]{:S(2)}) async-start(), calls=%async_computation.8 | async-start | bytes 524288 | tf_op jit(solution)/shard_map/psum | solution.py:37
  585.5 113.6 %all-reduce.35.cloned.1.call-start = ((), (), s32[]{:S(2)}) async-start(), calls=%async_computation.9 | async-start | bytes 1048576 | tf_op jit(solution)/shard_map/psum | solution.py:41
  626.6 131.0 %all-reduce.37.cloned.1.call-start = ((), (), s32[]{:S(2)}) async-start(), calls=%async_computation.10 | async-start | bytes 524288 | tf_op jit(solution)/shard_map/psum | solution.py:37
  726.8 112.7 %all-reduce.39.cloned.1.call-start = ((), (), s32[]{:S(2)}) async-start(), calls=%async_computation.11 | async-start | bytes 1048576 | tf_op jit(solution)/shard_map/psum | solution.py:41
  767.0 120.2 %all-reduce.41.cloned.1.call-start = ((), (), s32[]{:S(2)}) async-start(), calls=%async_computation.12 | async-start | bytes 524288 | tf_op jit(solution)/shard_map/psum | solution.py:75
  855.8 162.4 %copy-start.6 = (f32[1024,64]{0,1:T(8,128)S(1)}, f32[1024,64]{0,1:T(8,128)}, u32[]{:S(2)}) copy-start(f32[1024,64]{0,1:T(8,128)} %all-reduce.37.cloned.1.call-done) | copy-start | bytes 786436
  855.8 118.0 %all-reduce.43.cloned.1.call-start = ((), (), s32[]{:S(2)}) async-start(), calls=%async_computation.13 | async-start | bytes 2097152 | tf_op jit(solution)/shard_map/psum | solution.py:41
  895.5 204.7 %copy-start.4 = (f32[2048,64]{0,1:T(8,128)S(1)}, f32[2048,64]{0,1:T(8,128)}, u32[]{:S(2)}) copy-start(f32[2048,64]{0,1:T(8,128)} %all-reduce.35.cloned.1.call-done) | copy-start | bytes 1572868
  895.5 122.7 %all-reduce.45.cloned.1.call-start = ((), (), s32[]{:S(2)}) async-start(), calls=%async_computation.14 | async-start | bytes 524288 | tf_op jit(solution)/shard_map/psum | solution.py:37
  986.5 113.7 %all-reduce.47.cloned.1.call-start = ((), (), s32[]{:S(2)}) async-start(), calls=%async_computation.15 | async-start | bytes 1048576 | tf_op jit(solution)/shard_map/psum | solution.py:41
  1027.7 123.0 %all-reduce.49.cloned.1.call-start = ((), (), s32[]{:S(2)}) async-start(), calls=%async_computation.16 | async-start | bytes 524288 | tf_op jit(solution)/shard_map/psum | solution.py:37
  1107.8 52.3 %copy-start.5 = (f32[2048,64]{0,1:T(8,128)}, f32[2048,64]{0,1:T(8,128)S(1)}, u32[]{:S(2)}) copy-start(f32[2048,64]{0,1:T(8,128)S(1)} %multiply_add_fusion) | copy-start | bytes 1572868
  1119.1 113.6 %all-reduce.51.cloned.1.call-start = ((), (), s32[]{:S(2)}) async-start(), calls=%async_computation.17 | async-start | bytes 1048576 | tf_op jit(solution)/shard_map/psum | solution.py:41
Sparse Core Ops, SparseCore 0:
  12.7 76.0 all-gather.1
  109.9 76.3 all-reduce.18
  199.2 31.5 all-reduce.20
  240.3 72.3 all-reduce.22
  325.1 31.2 all-reduce.24
  366.0 72.3 all-reduce.26
  454.8 31.2 all-reduce.28
  494.5 78.1 all-reduce.30
  585.6 31.5 all-reduce.32
  626.7 72.3 all-reduce.34
  726.9 30.6 all-reduce.36
  767.1 72.3 all-reduce.38
  855.9 31.2 all-reduce.40
  895.6 78.1 all-reduce.42
  986.6 31.5 all-reduce.44
  1027.8 72.3 all-reduce.46
  1119.2 31.4 all-reduce.48
  1160.2 72.3 all-reduce.50
where the time goes:
time: 1250 us; the launch traced here: 1240 us
  waiting for transfers between devices  992 us (79%)
  matrix products  194 us (16%)
  blocking collectives  18.6 us (1%)
  between operations  14.9 us (1%)
    psum x9, waiting for transfers between devices, row_total(): return lax.psum(values, 'row')  667 us
    psum x6, waiting for transfers between devices, col_total(): return lax.psum(values, 'col')  189 us
    dot_general x8, matrix products, times_matrix(): jnp.dot(matrix, vectors, precision=HIGHEST, preferred_element_type=jnp.fl...  107 us
    dot_general x9, matrix products, contract_rows(): lax.dot_general(matrix, vectors, (((0,), (0,)), ((), ())), precision=HIGH...  80.7 us
    all_gather x1, waiting for transfers between devices, shards(): landmarks = lax.all_gather(owned, 'row', axis=0, tiled=True)  74.1 us
    psum x2, waiting for transfers between devices, shards(): lax.psum(times_matrix(kernel, lifted).astype(jnp.bfloat16), 'col')  62.7 us
  transfers between devices with their start and end apart: 18, of which 18 were waited for; matrix products, arithmetic and copies ran while one was open for 0% of the time, Pallas kernels for 0%

commit v1 on v0

--- a/solution.py
+++ b/solution.py
@@ -72,9 +72,9 @@
     for iteration in range(ITERS):
         mixed_in = col_total(times_matrix(factor_a, direction))
         lifted = row_total(contract_rows(factor_t, mixed_in))
-        example_vals = lax.psum(times_matrix(kernel, lifted).astype(jnp.bfloat16), "col").astype(
-            jnp.float32
-        )
+        example_vals = jnp.sum(
+            lax.all_gather(times_matrix(kernel, lifted).astype(jnp.bfloat16), "col"), axis=0
+        ).astype(jnp.float32)
         local_back = contract_rows(kernel, example_vals)
         back = row_total(local_back)
         curvature = None

time: 1250 us -> 1180 us (0.944)
  waiting for transfers between devices: 992 us -> 927 us
  matrix products: 194 us -> 177 us
  blocking collectives: 18.6 us -> 32.9 us
    psum x2 -> x0, waiting for transfers between devices: 62.7 us -> none  [shards(): lax.psum(times_matrix(kernel, lifted).astype(jnp.bfloat16), 'col')]
    dot_general x8, matrix products: 107 us -> 91.7 us  [times_matrix(): jnp.dot(matrix, vectors, precision=HIGHEST, preferred_element_type=jnp.fl...]
    all_gather x0 -> x2, blocking collectives: none -> 14.3 us  [shards(): lax.all_gather(times_matrix(kernel, lifted).astype(jnp.bfloat16), 'col')]
  transfers between devices with their start and end apart: 18 -> 16, of which waited for: 18 -> 16; matrix products, arithmetic and copies ran while one was open for 0% -> 0% of each run, Pallas kernels for 0% -> 0%
where the time goes in v1:
time: 1180 us
  waiting for transfers between devices  927 us (79%)
  matrix products  177 us (15%)
  blocking collectives  32.9 us (3%)
  between operations  14.6 us (1%)
  other arithmetic  12.5 us (1%)
    psum x9, waiting for transfers between devices, row_total(): return lax.psum(values, 'row')  664 us
    psum x6, waiting for transfers between devices, col_total(): return lax.psum(values, 'col')  189 us
    dot_general x8, matrix products, times_matrix(): jnp.dot(matrix, vectors, precision=HIGHEST, preferred_element_type=jnp.fl...  91.7 us
    dot_general x9, matrix products, contract_rows(): lax.dot_general(matrix, vectors, (((0,), (0,)), ((), ())), precision=HIGH...  78.8 us
    all_gather x1, waiting for transfers between devices, shards(): landmarks = lax.all_gather(owned, 'row', axis=0, tiled=True)  74.1 us
  transfers between devices with their start and end apart: 16, of which 16 were waited for; matrix products, arithmetic and copies ran while one was open for 0% of the time, Pallas kernels for 0%

profile of v1, /device:TPU:0, one launch (start us, length us, event | category | flops | bytes accessed | tf_op | source)
XLA Modules:
  0.0 1175.3 jit_solution(16420200129040761458)
XLA Ops:
  7.2 0.9 compare_and_fusion
  8.2 3.4 gather_fusion
  12.6 2.1 multiply_reduce_fusion.1
  14.7 74.1 %all-gather.4.cloned.1.call-done = bf16[2048,1024]{1,0:T(8,128)(2,1)} async-done(((bf16[256,1024]{1,0:T(8,128)(2,1)}), bf16[2048,1024]{1,0:T(8,128)(2,1)}) %all-gather.4.cloned.1.call-update) | async-done | bytes 4194320 | tf_op jit(solution)/shard_map/all_gather | solution.py:60
  88.8 3.1 multiply_reduce_fusion
  91.9 6.9 fusion.2
  98.8 3.2 copy-done.1
  102.0 7.7 fusion.21
  110.0 76.3 %all-reduce.17.cloned.1.call-done = f32[2048,64]{1,0:T(8,128)} async-done(((f32[2048,64]{1,0:T(8,128)}), f32[2048,64]{1,0:T(8,128)}) %all-reduce.17.cloned.1.call-update) | async-done | bytes 524304 | tf_op jit(solution)/shard_map/psum | solution.py:41
  186.3 12.7 %convolution_bitcast_fusion.11 = f32[1024,64]{0,1:T(8,128)} fusion(f32[2048,64]{1,0:T(8,128)} %all-reduce.17.cloned.1.call-done, f32[1024,2048]{1,0:T(8,128)} %bitcast.76), kind=kOutput, calls=%fused_computation.18 | convolution fusion | flops 1610612736 | bytes 9175040 | tf_op jit(solution)/shard_map/dot_general | solution.py:33
  199.1 31.7 %all-reduce.19.cloned.1.call-done = f32[1024,64]{0,1:T(8,128)} async-done(((f32[1024,64]{0,1:T(8,128)}), f32[1024,64]{0,1:T(8,128)}) %all-reduce.19.cloned.1.call-update) | async-done | bytes 262160 | tf_op jit(solution)/shard_map/psum | solution.py:37
  230.7 9.4 convolution_bitcast_fusion.5
  240.6 72.1 %all-reduce.21.cloned.1.call-done = f32[2048,64]{0,1:T(8,128)} async-done(((f32[2048,64]{0,1:T(8,128)}), f32[2048,64]{0,1:T(8,128)}) %all-reduce.21.cloned.1.call-update) | async-done | bytes 524304 | tf_op jit(solution)/shard_map/psum | solution.py:41
  312.7 12.3 %convolution_bitcast_fusion.8 = f32[1024,64]{0,1:T(8,128)} fusion(f32[1024,2048]{1,0:T(8,128)} %bitcast.71, f32[2048,64]{0,1:T(8,128)} %all-reduce.21.cloned.1.call-done), kind=kOutput, calls=%fused_computation.15 | convolution fusion | flops 1610743808 | bytes 9175040 | tf_op jit(solution)/shard_map/dot_general | solution.py:33
  325.1 31.3 %all-reduce.23.cloned.1.call-done = f32[1024,64]{0,1:T(8,128)} async-done(((f32[1024,64]{0,1:T(8,128)}), f32[1024,64]{0,1:T(8,128)}) %all-reduce.23.cloned.1.call-update) | async-done | bytes 262160 | tf_op jit(solution)/shard_map/psum | solution.py:37
  356.4 9.4 convolution_bitcast_fusion.4
  366.1 72.3 %all-reduce.25.cloned.1.call-done = f32[2048,64]{0,1:T(8,128)} async-done(((f32[2048,64]{0,1:T(8,128)}), f32[2048,64]{0,1:T(8,128)}) %all-reduce.25.cloned.1.call-update) | async-done | bytes 524304 | tf_op jit(solution)/shard_map/psum | solution.py:41
  438.4 8.8 convolution_convert_fusion.1
  447.2 7.1 all-gather
  455.4 7.3 fusion.22
  462.9 76.5 %all-reduce.27.cloned.1.call-done = f32[2048,64]{1,0:T(8,128)} async-done(((f32[2048,64]{1,0:T(8,128)}), f32[2048,64]{1,0:T(8,128)}) %all-reduce.27.cloned.1.call-update) | async-done | bytes 524304 | tf_op jit(solution)/shard_map/psum | solution.py:41
  539.5 12.7 %convolution_bitcast_fusion.10 = f32[1024,64]{0,1:T(8,128)} fusion(f32[2048,64]{1,0:T(8,128)} %all-reduce.27.cloned.1.call-done, f32[1024,2048]{1,0:T(8,128)} %bitcast.78), kind=kOutput, calls=%fused_computation.17 | convolution fusion | flops 1610612736 | bytes 9175040 | tf_op jit(solution)/shard_map/dot_general | solution.py:33
  552.3 31.7 %all-reduce.29.cloned.1.call-done = f32[1024,64]{0,1:T(8,128)} async-done(((f32[1024,64]{0,1:T(8,128)}), f32[1024,64]{0,1:T(8,128)}) %all-reduce.29.cloned.1.call-update) | async-done | bytes 262160 | tf_op jit(solution)/shard_map/psum | solution.py:37
  583.9 9.4 convolution_bitcast_fusion.3
  593.4 72.4 %all-reduce.31.cloned.1.call-done = f32[2048,64]{0,1:T(8,128)} async-done(((f32[2048,64]{0,1:T(8,128)}), f32[2048,64]{0,1:T(8,128)}) %all-reduce.31.cloned.1.call-update) | async-done | bytes 524304 | tf_op jit(solution)/shard_map/psum | solution.py:41
  665.8 1.2 multiply_reduce_fusion.4
  667.1 5.7 all-reduce
  672.7 1.3 multiply_reduce_fusion.3
  674.0 7.0 psum.143
  681.1 12.4 %convolution_bitcast_fusion.7 = f32[1024,64]{0,1:T(8,128)} fusion(f32[1024,2048]{1,0:T(8,128)} %bitcast.73, f32[2048,64]{0,1:T(8,128)S(1)} %copy-done.2, f32[2048,64]{0,1:T(8,128)} %all-reduce.31.cloned.1.call-done, f32[64]{0:T(128)S(1)} %fusion.15, f32[64]{0:T(128)S(1)} %get-tuple-element.7), kind=kOutput, calls=%fused_computation.14 | convolution fusion | flops 1611268096 | bytes 9699840 | tf_op jit(solution)/shard_map/dot_general | solution.py:33
  693.5 30.8 %all-reduce.33.cloned.1.call-done = f32[1024,64]{0,1:T(8,128)} async-done(((f32[1024,64]{0,1:T(8,128)}), f32[1024,64]{0,1:T(8,128)}) %all-reduce.33.cloned.1.call-update) | async-done | bytes 262160 | tf_op jit(solution)/shard_map/psum | solution.py:37
  724.3 9.4 convolution_bitcast_fusion.2
  734.0 72.2 %all-reduce.35.cloned.1.call-done = f32[2048,64]{0,1:T(8,128)} async-done(((f32[2048,64]{0,1:T(8,128)}), f32[2048,64]{0,1:T(8,128)}) %all-reduce.35.cloned.1.call-update) | async-done | bytes 524304 | tf_op jit(solution)/shard_map/psum | solution.py:41
  806.2 8.8 convolution_convert_fusion
  815.0 7.1 all-gather.1
  823.2 7.3 fusion.23
  830.9 76.8 %all-reduce.37.cloned.1.call-done = f32[2048,64]{1,0:T(8,128)} async-done(((f32[2048,64]{1,0:T(8,128)}), f32[2048,64]{1,0:T(8,128)}) %all-reduce.37.cloned.1.call-update) | async-done | bytes 524304 | tf_op jit(solution)/shard_map/psum | solution.py:41
  907.6 12.7 %convolution_bitcast_fusion.9 = f32[1024,64]{0,1:T(8,128)} fusion(f32[2048,64]{1,0:T(8,128)} %all-reduce.37.cloned.1.call-done, f32[1024,2048]{1,0:T(8,128)} %bitcast.80), kind=kOutput, calls=%fused_computation.16 | convolution fusion | flops 1610612736 | bytes 9175040 | tf_op jit(solution)/shard_map/dot_general | solution.py:33
  920.4 31.6 %all-reduce.39.cloned.1.call-done = f32[1024,64]{0,1:T(8,128)} async-done(((f32[1024,64]{0,1:T(8,128)}), f32[1024,64]{0,1:T(8,128)}) %all-reduce.39.cloned.1.call-update) | async-done | bytes 262160 | tf_op jit(solution)/shard_map/psum | solution.py:37
  952.1 9.4 convolution_bitcast_fusion.1
  961.6 72.4 %all-reduce.41.cloned.1.call-done = f32[2048,64]{0,1:T(8,128)} async-done(((f32[2048,64]{0,1:T(8,128)}), f32[2048,64]{0,1:T(8,128)}) %all-reduce.41.cloned.1.call-update) | async-done | bytes 524304 | tf_op jit(solution)/shard_map/psum | solution.py:41
  1034.0 1.3 multiply_reduce_fusion.2
  1035.3 5.9 psum.149
  1041.6 11.3 convolution_bitcast_fusion.6
  1052.9 31.6 %all-reduce.43.cloned.1.call-done = f32[1024,64]{0,1:T(8,128)} async-done(((f32[1024,64]{0,1:T(8,128)}), f32[1024,64]{0,1:T(8,128)}) %all-reduce.43.cloned.1.call-update) | async-done | bytes 262160 | tf_op jit(solution)/shard_map/psum | solution.py:37
  1084.5 9.4 convolution_bitcast_fusion
  1093.9 72.5 %all-reduce.45.cloned.1.call-done = f32[2048,64]{0,1:T(8,128)} async-done(((f32[2048,64]{0,1:T(8,128)}), f32[2048,64]{0,1:T(8,128)}) %all-reduce.45.cloned.1.call-update) | async-done | bytes 524304 | tf_op jit(solution)/shard_map/psum | solution.py:41
  1166.4 1.9 copy.22
  (57 shorter events, 5.7 us)
Async XLA Ops:
  7.2 94.8 %copy-start = (f32[1024,64]{0,1:T(8,128)S(1)}, f32[1024,64]{0,1:T(8,128)}, u32[]{:S(2)}) copy-start(f32[1024,64]{0,1:T(8,128)} %param.6) | copy-start | bytes 786436
  7.2 84.7 %copy-start.3 = (bf16[1024,1024]{1,0:T(8,128)(2,1)S(1)}, bf16[1024,1024]{1,0:T(8,128)(2,1)}, u32[]{:S(2)}) copy-start(bf16[1024,1024]{1,0:T(8,128)(2,1)} %param.5) | copy-start | bytes 6291460
  7.2 81.6 %all-gather.4.cloned.1.call-start = ((), (), s32[]{:S(2)}) async-start(), calls=%async_computation | async-start | bytes 4718592 | tf_op jit(solution)/shard_map/all_gather | solution.py:60
  12.5 173.8 %all-reduce.17.cloned.1.call-start = ((), (), s32[]{:S(2)}) async-start(), calls=%async_computation.1 | async-start | bytes 2097152 | tf_op jit(solution)/shard_map/psum | solution.py:41
  98.7 3.2 copy-start.1
  109.7 121.0 %all-reduce.19.cloned.1.call-start = ((), (), s32[]{:S(2)}) async-start(), calls=%async_computation.2 | async-start | bytes 524288 | tf_op jit(solution)/shard_map/psum | solution.py:37
  199.0 113.7 %all-reduce.21.cloned.1.call-start = ((), (), s32[]{:S(2)}) async-start(), calls=%async_computation.3 | async-start | bytes 1048576 | tf_op jit(solution)/shard_map/psum | solution.py:41
  240.2 116.2 %all-reduce.23.cloned.1.call-start = ((), (), s32[]{:S(2)}) async-start(), calls=%async_computation.4 | async-start | bytes 524288 | tf_op jit(solution)/shard_map/psum | solution.py:37
  325.0 113.4 %all-reduce.25.cloned.1.call-start = ((), (), s32[]{:S(2)}) async-start(), calls=%async_computation.5 | async-start | bytes 1048576 | tf_op jit(solution)/shard_map/psum | solution.py:41
  365.8 173.6 %all-reduce.27.cloned.1.call-start = ((), (), s32[]{:S(2)}) async-start(), calls=%async_computation.6 | async-start | bytes 2097152 | tf_op jit(solution)/shard_map/psum | solution.py:41
  455.4 128.6 %copy-start.7 = (f32[1024,64]{0,1:T(8,128)S(1)}, f32[1024,64]{0,1:T(8,128)}, u32[]{:S(2)}) copy-start(f32[1024,64]{0,1:T(8,128)} %all-reduce.23.cloned.1.call-done) | copy-start | bytes 786436
  462.7 203.2 %copy-start.2 = (f32[2048,64]{0,1:T(8,128)S(1)}, f32[2048,64]{0,1:T(8,128)}, u32[]{:S(2)}) copy-start(f32[2048,64]{0,1:T(8,128)} %all-reduce.21.cloned.1.call-done) | copy-start | bytes 1572868
  462.7 121.3 %all-reduce.29.cloned.1.call-start = ((), (), s32[]{:S(2)}) async-start(), calls=%async_computation.7 | async-start | bytes 524288 | tf_op jit(solution)/shard_map/psum | solution.py:37
  552.2 113.6 %all-reduce.31.cloned.1.call-start = ((), (), s32[]{:S(2)}) async-start(), calls=%async_computation.8 | async-start | bytes 1048576 | tf_op jit(solution)/shard_map/psum | solution.py:41
  593.4 131.0 %all-reduce.33.cloned.1.call-start = ((), (), s32[]{:S(2)}) async-start(), calls=%async_computation.9 | async-start | bytes 524288 | tf_op jit(solution)/shard_map/psum | solution.py:37
  693.5 112.7 %all-reduce.35.cloned.1.call-start = ((), (), s32[]{:S(2)}) async-start(), calls=%async_computation.10 | async-start | bytes 1048576 | tf_op jit(solution)/shard_map/psum | solution.py:41
  733.8 173.8 %all-reduce.37.cloned.1.call-start = ((), (), s32[]{:S(2)}) async-start(), calls=%async_computation.11 | async-start | bytes 2097152 | tf_op jit(solution)/shard_map/psum | solution.py:41
  823.2 128.9 %copy-start.6 = (f32[1024,64]{0,1:T(8,128)S(1)}, f32[1024,64]{0,1:T(8,128)}, u32[]{:S(2)}) copy-start(f32[1024,64]{0,1:T(8,128)} %all-reduce.33.cloned.1.call-done) | copy-start | bytes 786436
  830.6 203.4 %copy-start.4 = (f32[2048,64]{0,1:T(8,128)S(1)}, f32[2048,64]{0,1:T(8,128)}, u32[]{:S(2)}) copy-start(f32[2048,64]{0,1:T(8,128)} %all-reduce.31.cloned.1.call-done) | copy-start | bytes 1572868
  830.6 121.5 %all-reduce.39.cloned.1.call-start = ((), (), s32[]{:S(2)}) async-start(), calls=%async_computation.12 | async-start | bytes 524288 | tf_op jit(solution)/shard_map/psum | solution.py:37
  920.4 113.6 %all-reduce.41.cloned.1.call-start = ((), (), s32[]{:S(2)}) async-start(), calls=%async_computation.13 | async-start | bytes 1048576 | tf_op jit(solution)/shard_map/psum | solution.py:41
  961.5 123.0 %all-reduce.43.cloned.1.call-start = ((), (), s32[]{:S(2)}) async-start(), calls=%async_computation.14 | async-start | bytes 524288 | tf_op jit(solution)/shard_map/psum | solution.py:37
  1041.6 52.3 %copy-start.5 = (f32[2048,64]{0,1:T(8,128)}, f32[2048,64]{0,1:T(8,128)S(1)}, u32[]{:S(2)}) copy-start(f32[2048,64]{0,1:T(8,128)S(1)} %multiply_add_fusion) | copy-start | bytes 1572868
  1052.9 113.6 %all-reduce.45.cloned.1.call-start = ((), (), s32[]{:S(2)}) async-start(), calls=%async_computation.15 | async-start | bytes 1048576 | tf_op jit(solution)/shard_map/psum | solution.py:41
Sparse Core Ops, SparseCore 0:
  12.7 76.0 all-gather.3
  109.9 76.3 all-reduce.16
  199.2 31.5 all-reduce.18
  240.3 72.3 all-reduce.20
  325.1 31.2 all-reduce.22
  366.0 72.3 all-reduce.24
  462.8 76.6 all-reduce.26
  552.3 31.5 all-reduce.28
  593.5 72.2 all-reduce.30
  693.6 30.6 all-reduce.32
  733.9 72.2 all-reduce.34
  830.7 76.8 all-reduce.36
  920.5 31.5 all-reduce.38
  961.6 72.3 all-reduce.40
  1053.0 31.4 all-reduce.42
  1094.0 72.3 all-reduce.44
